TPU v7x, 32 devices: a whole 2x2x4 slice. The times are simulated.
32 devices in a mesh: dp: 8 (over z, x), mp: 4 (over y, core).
Axes of the slice: x: 2, y: 2, z: 4, core: 2. Of those that a mesh axis runs over, the one named last changes fastest.
Arguments:
- activations: bfloat16 [4096, 3072], P('dp', 'mp'), may hold values from -6 to 6
- out_grads: bfloat16 [4096, 6144], P('dp', 'mp'), may hold values from -0.25 to 0.25
- error: bfloat16 [8, 3072, 6144], P('dp', 'mp'), may hold values from -8 to 8
- sketch: bfloat16 [6144, 64], replicated, may hold values from -0.078125 to 0.078125
- momentum: float32 [3072, 6144], P('mp', 'dp'), may hold values from -6 to 6
Outputs:
- error_new: bfloat16 [8, 3072, 6144], P('dp', 'mp')
- momentum_new: float32 [3072, 6144], P('mp', 'dp')
- next_sketch: bfloat16 [6144, 64], replicated
All inputs are finite; a program needn't handle non-finite values.
Results may differ from a plain program's by a relative error of at most 0.0057.
Values may be sent and summed in bfloat16 or wider, within the bound.
A program may use at most 64 MiB of HBM per device.

v0:
```python
import jax
import jax.numpy as jnp
from jax import lax
from jax.sharding import PartitionSpec as P

beta_decay = 0.9


def update_momentum(momentum, basis_rows, sketch_block):
    product = lax.dot_general(
        basis_rows, sketch_block, (((1,), (1,)), ((), ())), preferred_element_type=jnp.float32
    )
    return beta_decay * momentum + product


def local(activations, out_grads, error, sketch, momentum):
    own_error = error[0]
    product = lax.dot_general(
        activations,
        lax.all_gather(out_grads, "mp", axis=1, tiled=True),
        (((0,), (0,)), ((), ())),
        preferred_element_type=jnp.float32,
    )
    accumulated = (product + own_error.astype(jnp.float32)).astype(jnp.bfloat16)
    local_left = jnp.dot(accumulated, sketch, preferred_element_type=jnp.float32)
    left_sketch = lax.psum(local_left, "dp")
    gram_local = jnp.dot(
        left_sketch.T,
        left_sketch,
        precision=lax.Precision.HIGHEST,
        preferred_element_type=jnp.float32,
    )
    gram_matrix = lax.psum(gram_local, "mp")
    factor = jnp.linalg.cholesky(gram_matrix)
    basis_rows = jax.scipy.linalg.solve_triangular(factor, left_sketch.T, lower=True).T.astype(
        jnp.bfloat16
    )
    block_width = momentum.shape[1]
    local_right = lax.dot_general(
        accumulated, basis_rows, (((0,), (0,)), ((), ())), preferred_element_type=jnp.float32
    )
    right_sketch = lax.psum(local_right, ("dp", "mp"))
    next_sketch = right_sketch.astype(jnp.bfloat16)
    sketch_part = lax.dynamic_slice_in_dim(
        next_sketch, lax.axis_index("dp") * block_width, block_width, 0
    )
    momentum_new = update_momentum(momentum, basis_rows, sketch_part)
    decoded = lax.dot_general(
        basis_rows, next_sketch, (((1,), (1,)), ((), ())), preferred_element_type=jnp.float32
    )
    error_new = (accumulated.astype(jnp.float32) - decoded / lax.axis_size("dp")).astype(
        jnp.bfloat16
    )
    return (error_new[None], momentum_new, next_sketch)


def solution(mesh):
    in_specs = (P("dp", "mp"), P("dp", "mp"), P("dp", "mp", None), P(), P("mp", "dp"))
    out_specs = (P("dp", "mp", None), P("mp", "dp"), P())
    return jax.shard_map(local, mesh=mesh, in_specs=in_specs, out_specs=out_specs, check_vma=False)
```

profile of v0, /device:TPU:0, one launch (start us, length us, event | category | flops | bytes accessed | tf_op | source)
XLA Modules:
  0.0 249.4 jit_solution(14047941913646381180)
XLA Ops:
  7.2 0.0 copy-start
  7.2 0.0 all-gather.2.cloned.1.call-start
  7.2 0.7 all-gather.2.cloned.1.call-update
  7.9 0.0 copy-start.4
  7.9 0.0 all-reduce.3.cloned.1.call-start
  8.0 50.7 %all-gather.2.cloned.1.call-done = bf16[512,6144]{1,0:T(8,128)(2,1)} async-done(((bf16[512,1536]{1,0:T(8,128)(2,1)}), bf16[512,6144]{1,0:T(8,128)(2,1)}) %all-gather.2.cloned.1.call-update) | async-done | bytes 6291472 | tf_op jit(solution)/shard_map/all_gather | solution.py:20
  58.7 0.0 copy-done
  58.7 9.6 %fusion = bf16[768,6144]{1,0:T(8,128)(2,1)S(1)} fusion(bf16[1,768,6144]{2,1,0:T(8,128)(2,1)} %param.7, bf16[512,768]{1,0:T(8,128)(2,1)S(1)} %copy-done, bf16[512,6144]{1,0:T(8,128)(2,1)} %all-gather.2.cloned.1.call-done), kind=kOutput, calls=%fused_computation.1 | convolution fusion | flops 4845993984 | bytes 25952256 | tf_op jit(solution)/shard_map/dot_general | solution.py:18
  68.3 0.0 copy-start.1
  68.3 3.7 %copy-done.1 = bf16[768,6144]{1,0:T(8,128)(2,1)} copy-done((bf16[768,6144]{1,0:T(8,128)(2,1)}, bf16[768,6144]{1,0:T(8,128)(2,1)S(1)}, u32[]{:S(2)}) %copy-start.1) | copy-done | bytes 9437208
  72.1 0.0 copy-done.4
  72.1 3.7 %fusion.7 = f32[768,64]{0,1:T(8,128)} fusion(bf16[768,6144]{1,0:T(8,128)(2,1)S(1)} %fusion, bf16[6144,64]{0,1:T(8,128)(2,1)S(1)} %copy-done.4), kind=kOutput, calls=%fused_computation.17 | convolution fusion | flops 603979776 | bytes 10420224 | tf_op jit(solution)/shard_map/dot_general | solution.py:25
  75.7 0.0 all-reduce.3.cloned.1.call-update
  75.8 70.8 %all-reduce.3.cloned.1.call-done = f32[768,64]{0,1:T(8,128)} async-done(((f32[768,64]{0,1:T(8,128)}), f32[768,64]{0,1:T(8,128)}) %all-reduce.3.cloned.1.call-update) | async-done | bytes 196624 | tf_op jit(solution)/shard_map/psum | solution.py:26
  146.6 1.3 fusion.8
  147.9 10.3 %psum.22 = f32[64,64]{0,1:T(8,128)S(1)} all-reduce(f32[64,64]{0,1:T(8,128)S(1)} %fusion.8), channel_id=1, replica_groups=mesh['dp'=8,'mp'=4] {'mp'}, use_global_device_ids=true, to_apply=%region_1.0 | all-reduce | flops 4096 | bytes 32768 | tf_op jit(solution)/shard_map/psum | solution.py:33
  158.2 0.1 copy.9
  158.3 5.8 %cholesky.16 = f32[64,64]{1,0:T(8,128)S(1)} custom-call(f32[64,64]{1,0:T(8,128)S(1)} %fusion.5), custom_call_target="Cholesky" | custom-call | tf_op jit(solution)/shard_map/jit(cholesky)/cholesky | solution.py:34
  164.2 0.6 compare_reduce_fusion
  164.8 0.7 fusion.3
  165.5 4.9 %custom-call.7 = f32[1,64,64]{1,2,0:T(8,128)S(1)} custom-call(f32[1,64,64]{2,1,0:T(8,128)S(1)} %fusion.3), custom_call_target="InvertDiagBlocksLowerTriangular" | custom-call | tf_op jit(solution)/shard_map/jit(_solve_triangular)/triangular_solve | solution.py:35
  170.4 1.3 convolution_convert_fusion
  171.7 5.4 %fusion.9 = f32[6144,64]{0,1:T(8,128)S(1)} fusion(bf16[768,64]{0,1:T(8,128)(2,1)S(1)} %convolution_convert_fusion, bf16[768,6144]{1,0:T(8,128)(2,1)} %copy-done.1), kind=kOutput, calls=%fused_computation.19 | convolution fusion | flops 603979776 | bytes 11108352 | tf_op jit(solution)/shard_map/dot_general | solution.py:39
  177.1 55.7 %all-reduce.4 = bf16[6144,64]{0,1:T(8,128)(2,1)S(1)} all-reduce(f32[6144,64]{0,1:T(8,128)S(1)} %fusion.9), channel_id=1, replica_groups=mesh['dp'=8,'mp'=4] {'dp','mp'}, use_global_device_ids=true, to_apply=%region_4.5 | all-reduce | flops 393216 | bytes 2359296 | tf_op jit(solution)/shard_map/psum | solution.py:42
  232.8 0.0 copy-start.2
  232.8 0.0 copy-start.3
  232.8 7.8 %fusion.1 = bf16[1,768,6144]{2,1,0:T(8,128)(2,1)} fusion(bf16[768,64]{0,1:T(8,128)(2,1)S(1)} %convolution_convert_fusion, bf16[6144,64]{0,1:T(8,128)(2,1)S(1)} %all-reduce.4, bf16[768,6144]{1,0:T(8,128)(2,1)} %copy-done.1), kind=kOutput, calls=%fused_computation.3 | convolution fusion | flops 622854144 | bytes 19759104 | tf_op jit(solution)/shard_map/dot_general | solution.py:48
  240.7 0.0 copy-done.2
  240.7 0.0 copy-done.3
  240.7 1.9 multiply_add_fusion
  (2 shorter events, 0.0 us)
Async XLA Ops:
  7.2 51.5 %copy-start = (bf16[512,768]{1,0:T(8,128)(2,1)S(1)}, bf16[512,768]{1,0:T(8,128)(2,1)}, u32[]{:S(2)}) copy-start(bf16[512,768]{1,0:T(8,128)(2,1)} %param.5) | copy-start | bytes 2359300
  7.2 51.5 %all-gather.2.cloned.1.call-start = ((), (), s32[]{:S(2)}) async-start(), calls=%async_computation | async-start | bytes 7864320 | tf_op jit(solution)/shard_map/all_gather | solution.py:20
  7.9 64.2 %copy-start.4 = (bf16[6144,64]{0,1:T(8,128)(2,1)S(1)}, bf16[6144,64]{0,1:T(8,128)(2,1)}, u32[]{:S(2)}) copy-start(bf16[6144,64]{0,1:T(8,128)(2,1)} %param.8) | copy-start | bytes 2359300
  7.9 138.7 %all-reduce.3.cloned.1.call-start = ((), (), s32[]{:S(2)}) async-start(), calls=%async_computation.1 | async-start | bytes 393216 | tf_op jit(solution)/shard_map/psum | solution.py:26
  68.3 3.7 %copy-start.1 = (bf16[768,6144]{1,0:T(8,128)(2,1)}, bf16[768,6144]{1,0:T(8,128)(2,1)S(1)}, u32[]{:S(2)}) copy-start(bf16[768,6144]{1,0:T(8,128)(2,1)S(1)} %fusion) | copy-start | bytes 28311556
  232.8 7.8 %copy-start.2 = (bf16[6144,64]{0,1:T(8,128)(2,1)}, bf16[6144,64]{0,1:T(8,128)(2,1)S(1)}, u32[]{:S(2)}) copy-start(bf16[6144,64]{0,1:T(8,128)(2,1)S(1)} %all-reduce.4) | copy-start | bytes 2359300
  232.8 7.8 %copy-start.3 = (f32[768,768]{1,0:T(8,128)S(1)}, f32[768,768]{1,0:T(8,128)}, u32[]{:S(2)}) copy-start(f32[768,768]{1,0:T(8,128)} %param.9) | copy-start | bytes 7077892
Sparse Core Ops, SparseCore 0:
  9.5 49.0 all-gather.1
  75.9 70.6 all-reduce.2
where the time goes:
time: 250 us; the launch traced here: 249 us
  waiting for transfers between devices  122 us (49%)
  blocking collectives  66 us (26%)
  matrix products  31.1 us (12%)
  between operations  14.2 us (6%)
  other arithmetic  12.1 us (5%)
  local copies, waits for them, and re-layouts  3.84 us (2%)
    psum x1, waiting for transfers between devices, local(): left_sketch = lax.psum(local_left, 'dp')  70.8 us
    psum x1, blocking collectives, local(): right_sketch = lax.psum(local_right, ('dp', 'mp'))  55.7 us
    all_gather x1, waiting for transfers between devices, local(): lax.all_gather(out_grads, 'mp', axis=1, tiled=True)  50.7 us
    psum x1, blocking collectives, local(): gram_matrix = lax.psum(gram_local, 'mp')  10.3 us
    dot_general x1, matrix products, local(): lax.dot_general(activations, lax.all_gather(out_grads, 'mp', axis=1, tile...  9.64 us
    dot_general x1, matrix products, local(): lax.dot_general(basis_rows, next_sketch, (((1,), (1,)), ((), ())), prefer...  7.81 us
    another operation x3, other arithmetic, local(): factor = jnp.linalg.cholesky(gram_matrix)  6.52 us
    another operation x2, other arithmetic, local(): jax.scipy.linalg.solve_triangular(factor, left_sketch.T, lower=True)  5.55 us
  transfers between devices with their start and end apart: 2, of which 2 were waited for; matrix products, arithmetic and copies ran while one was open for 0% of the time, Pallas kernels for 0%

commit v1 on v0

--- a/solution.py
+++ b/solution.py
@@ -23,7 +23,11 @@
     )
     accumulated = (product + own_error.astype(jnp.float32)).astype(jnp.bfloat16)
     local_left = jnp.dot(accumulated, sketch, preferred_element_type=jnp.float32)
-    left_sketch = lax.psum(local_left, "dp")
+    left_sketch = local_left
+    for hop in (1, 2, 4):
+        left_sketch = left_sketch + lax.ppermute(
+            left_sketch, "dp", [(dev, dev ^ hop) for dev in range(8)]
+        )
     gram_local = jnp.dot(
         left_sketch.T,
         left_sketch,

time: 250 us -> 201 us (0.80)
  waiting for transfers between devices: 122 us -> 69.8 us
  starting transfers between devices: 0.08 us -> 5.59 us
  matrix products: 31.1 us -> 28.4 us
    psum x1 -> x0, waiting for transfers between devices: 70.8 us -> none  [local(): left_sketch = lax.psum(local_left, 'dp')]
    ppermute x0 -> x3, waiting for transfers between devices: none -> 18.3 us  [local(): lax.ppermute(left_sketch, 'dp', [(dev, dev ^ hop) for dev in range(8)])]
    ppermute x0 -> x3, starting transfers between devices: none -> 5.55 us  [local(): lax.ppermute(left_sketch, 'dp', [(dev, dev ^ hop) for dev in range(8)])]
  transfers between devices with their start and end apart: 2 -> 4, of which waited for: 2 -> 4; matrix products, arithmetic and copies ran while one was open for 0% -> 0% of each run, Pallas kernels for 0% -> 0%
where the time goes in v1:
time: 201 us; the launch traced here: 200 us
  waiting for transfers between devices  69.8 us (35%)
  blocking collectives  66.4 us (33%)
  matrix products  28.4 us (14%)
  between operations  14.2 us (7%)
  other arithmetic  12.2 us (6%)
  starting transfers between devices  5.59 us (3%)
  local copies, waits for them, and re-layouts  3.84 us (2%)
    psum x1, blocking collectives, local(): right_sketch = lax.psum(local_right, ('dp', 'mp'))  56.2 us
    all_gather x1, waiting for transfers between devices, local(): lax.all_gather(out_grads, 'mp', axis=1, tiled=True)  50.7 us
    ppermute x3, waiting for transfers between devices, local(): lax.ppermute(left_sketch, 'dp', [(dev, dev ^ hop) for dev in range(8)])  18.3 us
    psum x1, blocking collectives, local(): gram_matrix = lax.psum(gram_local, 'mp')  10.3 us
    dot_general x1, matrix products, local(): lax.dot_general(activations, lax.all_gather(out_grads, 'mp', axis=1, tile...  9.64 us
    dot_general x1, matrix products, local(): lax.dot_general(basis_rows, next_sketch, (((1,), (1,)), ((), ())), prefer...  7.81 us
    another operation x3, other arithmetic, local(): factor = jnp.linalg.cholesky(gram_matrix)  6.52 us
    ppermute x3, starting transfers between devices, local(): lax.ppermute(left_sketch, 'dp', [(dev, dev ^ hop) for dev in range(8)])  5.55 us
  transfers between devices with their start and end apart: 4, of which 4 were waited for; matrix products, arithmetic and copies ran while one was open for 0% of the time, Pallas kernels for 0%

profile of v1, /device:TPU:0, one launch (start us, length us, event | category | flops | bytes accessed | tf_op | source)
XLA Modules:
  0.0 200.4 jit_solution(16785870263749307749)
XLA Ops:
  7.2 0.0 copy-start
  7.2 0.0 all-gather.2.cloned.1.call-start
  7.2 0.7 all-gather.2.cloned.1.call-update
  7.9 0.0 copy-start.4
  7.9 50.7 %all-gather.2.cloned.1.call-done = bf16[512,6144]{1,0:T(8,128)(2,1)} async-done(((bf16[512,1536]{1,0:T(8,128)(2,1)}), bf16[512,6144]{1,0:T(8,128)(2,1)}) %all-gather.2.cloned.1.call-update) | async-done | bytes 6291472 | tf_op jit(solution)/shard_map/all_gather | solution.py:20
  58.7 0.0 copy-done
  58.7 9.6 %fusion = bf16[768,6144]{1,0:T(8,128)(2,1)S(1)} fusion(bf16[1,768,6144]{2,1,0:T(8,128)(2,1)} %param.7, bf16[512,768]{1,0:T(8,128)(2,1)S(1)} %copy-done, bf16[512,6144]{1,0:T(8,128)(2,1)} %all-gather.2.cloned.1.call-done), kind=kOutput, calls=%fused_computation.1 | convolution fusion | flops 4845993984 | bytes 25952256 | tf_op jit(solution)/shard_map/dot_general | solution.py:18
  68.3 0.0 copy-start.1
  68.3 3.7 %copy-done.1 = bf16[768,6144]{1,0:T(8,128)(2,1)} copy-done((bf16[768,6144]{1,0:T(8,128)(2,1)}, bf16[768,6144]{1,0:T(8,128)(2,1)S(1)}, u32[]{:S(2)}) %copy-start.1) | copy-done | bytes 9437208
  72.1 0.0 copy-done.4
  72.1 3.0 %fusion.7 = f32[768,64]{0,1:T(8,128)S(1)} fusion(bf16[768,6144]{1,0:T(8,128)(2,1)S(1)} %fusion, bf16[6144,64]{0,1:T(8,128)(2,1)S(1)} %copy-done.4), kind=kOutput, calls=%fused_computation.17 | convolution fusion | flops 603979776 | bytes 10420224 | tf_op jit(solution)/shard_map/dot_general | solution.py:25
  75.0 1.5 collective-permute-start
  76.6 5.6 %collective-permute-done = f32[768,64]{0,1:T(8,128)S(1)} collective-permute-done((f32[768,64]{0,1:T(8,128)S(1)}, f32[768,64]{0,1:T(8,128)S(1)}, u32[]{:S(2)}, u32[]{:S(2)}) %collective-permute-start) | collective-permute-done | bytes 196640 | tf_op jit(solution)/shard_map/ppermute | solution.py:28
  82.2 1.6 collective-permute-start.1
  83.7 4.7 %collective-permute-done.1 = f32[768,64]{0,1:T(8,128)S(1)} collective-permute-done((f32[768,64]{0,1:T(8,128)S(1)}, f32[768,64]{0,1:T(8,128)S(1)}, u32[]{:S(2)}, u32[]{:S(2)}) %collective-permute-start.1) | collective-permute-done | bytes 196640 | tf_op jit(solution)/shard_map/ppermute | solution.py:28
  88.5 2.5 %collective-permute-start.2 = (f32[768,64]{0,1:T(8,128)S(1)}, f32[768,64]{0,1:T(8,128)S(1)}, u32[]{:S(2)}, u32[]{:S(2)}) collective-permute-start(f32[768,64]{0,1:T(8,128)S(1)} %add.36), channel_id=1, source_target_pairs={{0,16},{4,20},{8,24},{12,28},{16,0},{20,4},{24,8},{28,12},{1,17},{... | collective-permute-start | bytes 589832 | tf_op jit(solution)/shard_map/ppermute | solution.py:28
  90.9 8.1 %collective-permute-done.2 = f32[768,64]{0,1:T(8,128)S(1)} collective-permute-done((f32[768,64]{0,1:T(8,128)S(1)}, f32[768,64]{0,1:T(8,128)S(1)}, u32[]{:S(2)}, u32[]{:S(2)}) %collective-permute-start.2) | collective-permute-done | bytes 196640 | tf_op jit(solution)/shard_map/ppermute | solution.py:28
  99.0 0.3 fusion.8
  99.3 10.3 %psum.14 = f32[64,64]{0,1:T(8,128)S(1)} all-reduce(f32[64,64]{0,1:T(8,128)S(1)} %fusion.8), channel_id=1, replica_groups=mesh['dp'=8,'mp'=4] {'mp'}, use_global_device_ids=true, to_apply=%region_0.0 | all-reduce | flops 4096 | bytes 32768 | tf_op jit(solution)/shard_map/psum | solution.py:37
  109.6 0.1 copy.9
  109.7 5.8 %cholesky.16 = f32[64,64]{1,0:T(8,128)S(1)} custom-call(f32[64,64]{1,0:T(8,128)S(1)} %fusion.5), custom_call_target="Cholesky" | custom-call | tf_op jit(solution)/shard_map/jit(cholesky)/cholesky | solution.py:38
  115.6 0.6 compare_reduce_fusion
  116.2 0.7 fusion.3
  116.9 4.9 %custom-call.7 = f32[1,64,64]{1,2,0:T(8,128)S(1)} custom-call(f32[1,64,64]{2,1,0:T(8,128)S(1)} %fusion.3), custom_call_target="InvertDiagBlocksLowerTriangular" | custom-call | tf_op jit(solution)/shard_map/jit(_solve_triangular)/triangular_solve | solution.py:39
  121.8 0.4 convolution_convert_fusion
  122.2 5.4 %fusion.9 = f32[6144,64]{0,1:T(8,128)S(1)} fusion(bf16[768,64]{0,1:T(8,128)(2,1)S(1)} %convolution_convert_fusion, bf16[768,6144]{1,0:T(8,128)(2,1)} %copy-done.1), kind=kOutput, calls=%fused_computation.19 | convolution fusion | flops 603979776 | bytes 11108352 | tf_op jit(solution)/shard_map/dot_general | solution.py:43
  127.6 56.2 %all-reduce.1 = bf16[6144,64]{0,1:T(8,128)(2,1)S(1)} all-reduce(f32[6144,64]{0,1:T(8,128)S(1)} %fusion.9), channel_id=1, replica_groups=mesh['dp'=8,'mp'=4] {'dp','mp'}, use_global_device_ids=true, to_apply=%region_3.4 | all-reduce | flops 393216 | bytes 2359296 | tf_op jit(solution)/shard_map/psum | solution.py:46
  183.8 0.0 copy-start.2
  183.8 0.0 copy-start.3
  183.8 7.8 %fusion.1 = bf16[1,768,6144]{2,1,0:T(8,128)(2,1)} fusion(bf16[768,64]{0,1:T(8,128)(2,1)S(1)} %convolution_convert_fusion, bf16[6144,64]{0,1:T(8,128)(2,1)S(1)} %all-reduce.1, bf16[768,6144]{1,0:T(8,128)(2,1)} %copy-done.1), kind=kOutput, calls=%fused_computation.3 | convolution fusion | flops 622854144 | bytes 19759104 | tf_op jit(solution)/shard_map/dot_general | solution.py:52
  191.6 0.0 copy-done.2
  191.6 0.0 copy-done.3
  191.6 1.9 multiply_add_fusion
  (5 shorter events, 0.1 us)
Async XLA Ops:
  7.2 51.5 %copy-start = (bf16[512,768]{1,0:T(8,128)(2,1)S(1)}, bf16[512,768]{1,0:T(8,128)(2,1)}, u32[]{:S(2)}) copy-start(bf16[512,768]{1,0:T(8,128)(2,1)} %param.5) | copy-start | bytes 2359300
  7.2 51.5 %all-gather.2.cloned.1.call-start = ((), (), s32[]{:S(2)}) async-start(), calls=%async_computation | async-start | bytes 7864320 | tf_op jit(solution)/shard_map/all_gather | solution.py:20
  7.9 64.2 %copy-start.4 = (bf16[6144,64]{0,1:T(8,128)(2,1)S(1)}, bf16[6144,64]{0,1:T(8,128)(2,1)}, u32[]{:S(2)}) copy-start(bf16[6144,64]{0,1:T(8,128)(2,1)} %param.8) | copy-start | bytes 2359300
  68.3 3.7 %copy-start.1 = (bf16[768,6144]{1,0:T(8,128)(2,1)}, bf16[768,6144]{1,0:T(8,128)(2,1)S(1)}, u32[]{:S(2)}) copy-start(bf16[768,6144]{1,0:T(8,128)(2,1)S(1)} %fusion) | copy-start | bytes 28311556
  75.0 7.1 %collective-permute-start = (f32[768,64]{0,1:T(8,128)S(1)}, f32[768,64]{0,1:T(8,128)S(1)}, u32[]{:S(2)}, u32[]{:S(2)}) collective-permute-start(f32[768,64]{0,1:T(8,128)S(1)} %fusion.7), channel_id=1, source_target_pairs={{0,4},{4,0},{8,12},{12,8},{16,20},{20,16},{24,28},{28,24},{1,5},{5... | collective-permute-start | bytes 589832 | tf_op jit(solution)/shard_map/ppermute | solution.py:28
  82.2 6.3 %collective-permute-start.1 = (f32[768,64]{0,1:T(8,128)S(1)}, f32[768,64]{0,1:T(8,128)S(1)}, u32[]{:S(2)}, u32[]{:S(2)}) collective-permute-start(f32[768,64]{0,1:T(8,128)S(1)} %add.35), channel_id=1, source_target_pairs={{0,8},{4,12},{8,0},{12,4},{16,24},{20,28},{24,16},{28,20},{1,9},{5... | collective-permute-start | bytes 589832 | tf_op jit(solution)/shard_map/ppermute | solution.py:28
  88.5 10.5 %collective-permute-start.2 = (f32[768,64]{0,1:T(8,128)S(1)}, f32[768,64]{0,1:T(8,128)S(1)}, u32[]{:S(2)}, u32[]{:S(2)}) collective-permute-start(f32[768,64]{0,1:T(8,128)S(1)} %add.36), channel_id=1, source_target_pairs={{0,16},{4,20},{8,24},{12,28},{16,0},{20,4},{24,8},{28,12},{1,17},{... | collective-permute-start | bytes 589832 | tf_op jit(solution)/shard_map/ppermute | solution.py:28
  183.8 7.8 %copy-start.2 = (bf16[6144,64]{0,1:T(8,128)(2,1)}, bf16[6144,64]{0,1:T(8,128)(2,1)S(1)}, u32[]{:S(2)}) copy-start(bf16[6144,64]{0,1:T(8,128)(2,1)S(1)} %all-reduce.1) | copy-start | bytes 2359300
  183.8 7.8 %copy-start.3 = (f32[768,768]{1,0:T(8,128)S(1)}, f32[768,768]{1,0:T(8,128)}, u32[]{:S(2)}) copy-start(f32[768,768]{1,0:T(8,128)} %param.9) | copy-start | bytes 7077892
Sparse Core Ops, SparseCore 0:
  9.5 49.0 all-gather.1
